TPU v7x, 128 devices: a whole 4x4x4 slice. The times are simulated.
128 devices in a mesh: space: 16 (over y_hi, x, core), code: 4 (over z), clip: 2 (over y_lo).
Axes of the slice: x: 4, y: 4 (y_hi: 2, y_lo: 2; y = y_hi * 2 + y_lo), z: 4, core: 2. Of those that a mesh axis runs over, the one named last changes fastest.
Arguments:
- soft_weights: bfloat16 [2, 1024, 32, 8192], P('clip', 'space', None, 'code'), may hold values from 0.00029945374 to 0.029907227
- codebook: bfloat16 [8192, 256], P('code'), may hold values from -6 to 6
- kernel_one: bfloat16 [3, 3, 256, 512], replicated, may hold values from -0.125 to 0.125
- kernel_two: bfloat16 [3, 3, 512, 512], replicated, may hold values from -0.09375 to 0.09375
- cotangent: bfloat16 [2, 1024, 32, 512], P('clip', ('space', 'code')), may hold values from -16 to 16
Outputs:
- decoded: bfloat16 [2, 1024, 32, 512], P('clip', ('space', 'code'))
- grad_one: float32 [3, 3, 256, 512], P(None, None, None, ('space', 'code', 'clip'))
- grad_two: float32 [3, 3, 512, 512], P(None, None, None, ('space', 'code', 'clip'))
- grad_codebook: float32 [8192, 256], P('code')
All inputs are finite; a program needn't handle non-finite values.
Results may differ from a plain program's by a relative error of at most 0.02.
Values may be sent and summed in bfloat16 or wider, within the bound.
A program may use at most 192 MiB of HBM per device.

v0:
```python
import jax
import jax.numpy as jnp
from jax import lax
from jax.sharding import PartitionSpec as P


def with_halo(block, sides, width):
    for axis, dim in sides:
        count = lax.axis_size(axis)
        forward = [(i, i + 1) for i in range(count - 1)]
        backward = [(target, source) for source, target in forward]
        low = lax.ppermute(
            lax.slice_in_dim(block, block.shape[dim] - width, None, axis=dim), axis, forward
        )
        high = lax.ppermute(lax.slice_in_dim(block, 0, width, axis=dim), axis, backward)
        block = jnp.concatenate([low, block, high], axis=dim)
    return block


def extend(field):
    grown = with_halo(field, ((("space", "code"), 0),), 1)
    return jnp.pad(grown, ((0, 0), (1, 1), (0, 0)))


def taps_forward(padded, kernel):
    height = padded.shape[0] - 2
    breadth = padded.shape[1] - 2
    accum = jnp.zeros((height * breadth, kernel.shape[3]), jnp.float32)
    for first in range(3):
        for second in range(3):
            window = padded[first : first + height, second : second + breadth].reshape(
                height * breadth, -1
            )
            accum = accum + jnp.dot(
                window, kernel[first, second], preferred_element_type=jnp.float32
            )
    return accum.reshape(height, breadth, -1)


def taps_back(padded, kernel):
    height = padded.shape[0] - 2
    breadth = padded.shape[1] - 2
    accum = jnp.zeros((height * breadth, kernel.shape[2]), jnp.float32)
    for first in range(3):
        for second in range(3):
            window = padded[
                2 - first : 2 - first + height, 2 - second : 2 - second + breadth
            ].reshape(height * breadth, -1)
            accum = accum + jnp.dot(
                window, kernel[first, second].T, preferred_element_type=jnp.float32
            )
    return accum.reshape(height, breadth, -1)


def kernel_grad(padded, upstream):
    height = upstream.shape[0]
    breadth = upstream.shape[1]
    flat_up = upstream.reshape(height * breadth, -1)
    result = []
    for first in range(3):
        line = []
        for second in range(3):
            window = padded[first : first + height, second : second + breadth].reshape(
                height * breadth, -1
            )
            line.append(
                lax.dot_general(
                    window, flat_up, (((0,), (0,)), ((), ())), preferred_element_type=jnp.float32
                )
            )
        result.append(jnp.stack(line))
    return jnp.stack(result)


def on_device(soft_weights, codebook, kernel_one, kernel_two, cotangent):
    weights = soft_weights[0]
    upstream = cotangent[0]
    own_rows = upstream.shape[0]
    breadth = weights.shape[1]
    code_slice = weights.shape[2]
    partial_value = jnp.dot(
        weights.reshape(-1, code_slice), codebook, preferred_element_type=jnp.float32
    )
    partial_value = partial_value.reshape(weights.shape[0], breadth, -1)
    summed = lax.psum(partial_value, "code")
    owned = lax.dynamic_slice_in_dim(summed, lax.axis_index("code") * own_rows, own_rows, 0)
    embedded = owned.astype(jnp.bfloat16)
    embed_pad = extend(embedded)
    pre_one = taps_forward(embed_pad, kernel_one)
    hidden = jax.nn.silu(pre_one).astype(jnp.bfloat16)
    hidden_pad = extend(hidden)
    decoded = taps_forward(hidden_pad, kernel_two).astype(jnp.bfloat16)
    grad_hidden = taps_back(extend(upstream), kernel_two)
    sigma = jax.nn.sigmoid(pre_one)
    grad_pre = (grad_hidden * sigma * (1.0 + pre_one * (1.0 - sigma))).astype(jnp.bfloat16)
    grad_embedded = taps_back(extend(grad_pre), kernel_one).astype(jnp.bfloat16)
    piece = lax.all_gather(grad_embedded, "code", axis=0, tiled=True)
    code_terms = lax.dot_general(
        weights.reshape(-1, code_slice),
        piece.reshape(-1, piece.shape[2]),
        (((0,), (0,)), ((), ())),
        preferred_element_type=jnp.float32,
    )
    grad_codebook = lax.psum(code_terms.astype(jnp.bfloat16), ("space", "clip")).astype(jnp.float32)
    term_two = kernel_grad(hidden_pad, upstream)
    term_one = kernel_grad(embed_pad, grad_pre)
    grad_one, grad_two = (
        lax.psum_scatter(term_one, ("space", "code", "clip"), scatter_dimension=3, tiled=True),
        lax.psum_scatter(term_two, ("space", "code", "clip"), scatter_dimension=3, tiled=True),
    )
    return (decoded[None], grad_one, grad_two, grad_codebook)


def solution(mesh):
    in_specs = (
        P("clip", "space", None, "code"),
        P("code", None),
        P(),
        P(),
        P("clip", ("space", "code"), None, None),
    )
    out_specs = (
        P("clip", ("space", "code"), None, None),
        P(None, None, None, ("space", "code", "clip")),
        P(None, None, None, ("space", "code", "clip")),
        P("code", None),
    )
    return jax.shard_map(
        on_device, mesh=mesh, in_specs=in_specs, out_specs=out_specs, check_vma=False
    )
```

profile of v0, /device:TPU:1, one launch (start us, length us, event | category | flops | bytes accessed | tf_op | source)
XLA Modules:
  0.0 509.3 jit_solution(13997313864569233537)
XLA Ops:
  8.4 5.7 %fusion = f32[64,32,256]{2,1,0:T(8,128)S(1)} fusion(bf16[1,64,32,2048]{3,2,1,0:T(8,128)(2,1)} %param.5, bf16[2048,256]{1,0:T(8,128)(2,1)S(1)} %copy-done), kind=kOutput, calls=%fused_computation.1 | convolution fusion | flops 2147483648 | bytes 11534336 | tf_op jit(solution)/shard_map/dot_general | solution.py:81
  14.1 44.1 %all-reduce.14 = bf16[64,32,256]{2,1,0:T(8,128)(2,1)} all-reduce(f32[64,32,256]{2,1,0:T(8,128)S(1)} %fusion), channel_id=1, replica_groups=mesh['space'=16,'code'=4,'clip'=2] {'code'}, use_global_device_ids=true, to_apply=%region_0.0 | all-reduce | flops 524288 | bytes 3145728 | tf_op jit(solution)/shard_map/psum | solution.py:85
  59.4 1.9 collective-permute-start
  61.3 5.2 %collective-permute-start.1 = (bf16[1,32,256]{2,1,0:T(8,128)(2,1)S(1)}, bf16[1,32,256]{2,1,0:T(8,128)(2,1)S(1)}, u32[]{:S(2)}, u32[]{:S(2)}) collective-permute-start(bf16[1,32,256]{2,1,0:T(8,128)(2,1)S(1)} %get-tuple-element.55), channel_id=1, source_target_pairs={{2,0},{4,2},{6,4},{8,6},{10,8},{12,10},{14,12},{16,14},{18,16},{20... | collective-permute-start | bytes 49160 | tf_op jit(solution)/shard_map/ppermute | solution.py:15
  66.5 1.9 collective-permute-start.4
  68.5 4.9 collective-permute-start.5
  76.5 1.5 convolution_bitcast_fusion.4
  88.3 1.9 collective-permute-start.2
  90.2 4.9 collective-permute-start.3
  95.0 1.9 collective-permute-start.6
  97.0 5.0 collective-permute-start.7
  103.2 2.7 pad_maximum_fusion.1
  105.8 7.3 %copy.12 = f32[3,3,256,512]{2,1,0,3:T(4,128)} copy(f32[3,3,256,512]{3,2,1,0:T(8,128)} %pad_maximum_fusion.1) | data formatting | bytes 9437184 | tf_op jit(solution)/shard_map/stack | solution.py:72
  113.4 2.0 fusion.114
  127.8 3.4 maximum_bitcast_fusion
  131.2 27.6 %all-gather.2.cloned.1.call-done = bf16[64,32,256]{2,1,0:T(8,128)(2,1)} async-done(((bf16[16,32,256]{2,1,0:T(8,128)(2,1)}), bf16[64,32,256]{2,1,0:T(8,128)(2,1)}) %all-gather.2.cloned.1.call-update) | async-done | bytes 1048592 | tf_op jit(solution)/shard_map/all_gather | solution.py:97
  158.8 7.0 %fusion.2 = bf16[2048,256]{0,1:T(8,128)(2,1)} fusion(bf16[2048,256]{1,0:T(8,128)(2,1)} %bitcast.297, bf16[2048,2048]{1,0:T(8,128)(2,1)} %bitcast.275), kind=kOutput, calls=%fused_computation.8 | convolution fusion | flops 2148007936 | bytes 10485760 | tf_op jit(solution)/shard_map/dot_general | solution.py:98
  166.1 2.3 maximum_bitcast_fusion.2
  169.9 4.7 pad_maximum_fusion
  174.6 13.8 %copy.13 = f32[3,3,512,512]{2,1,0,3:T(4,128)} copy(f32[3,3,512,512]{3,2,1,0:T(8,128)} %pad_maximum_fusion) | data formatting | bytes 18874368 | tf_op jit(solution)/shard_map/stack | solution.py:72
  188.5 1.7 fusion.32
  190.2 1.5 fusion.14
  191.7 1.5 convolution_add_fusion.13
  193.2 1.5 convolution_add_fusion.12
  194.7 1.6 convolution_add_fusion.11
  196.3 1.5 convolution_add_fusion.10
  197.8 1.5 convolution_add_fusion.9
  199.3 1.5 convolution_add_fusion.8
  200.8 2.4 fusion.7
  203.2 70.1 %all-reduce.11.cloned.1.call-done = bf16[2048,256]{0,1:T(8,128)(2,1)} async-done(((bf16[2048,256]{0,1:T(8,128)(2,1)}), bf16[2048,256]{0,1:T(8,128)(2,1)}) %all-reduce.11.cloned.1.call-update) | async-done | bytes 1048592 | tf_op jit(solution)/shard_map/psum | solution.py:104
  273.2 2.6 copy.16
  275.8 223.9 %all-reduce.13.cloned.1.call-done = (f32[3,3,256,512]{2,1,0,3:T(4,128)}, f32[3,3,512,512]{2,1,0,3:T(4,128)}) async-done(((f32[3,3,256,512]{2,1,0,3:T(4,128)}, f32[3,3,512,512]{2,1,0,3:T(4,128)}), (f32[3,3,256,512]{2,1,0,3:T(4,128)}, f32[3,3,512,512]{2,1,0,3:T(4,128)})) %all-reduce.13.cloned.1.call-update) | async-done | bytes 14155792
  (136 shorter events, 33.8 us)
Async XLA Ops:
  7.2 151.6 %all-gather.2.cloned.1.call-start = ((), (), s32[]{:S(2)}) async-start(), calls=%async_computation | async-start | bytes 1310720 | tf_op jit(solution)/shard_map/all_gather | solution.py:97
  14.1 52.4 %copy-start.2 = (bf16[1,16,32,512]{3,2,1,0:T(8,128)(2,1)S(1)}, bf16[1,16,32,512]{3,2,1,0:T(8,128)(2,1)}, u32[]{:S(2)}) copy-start(bf16[1,16,32,512]{3,2,1,0:T(8,128)(2,1)} %param.9) | copy-start | bytes 1572868
  58.3 15.5 %copy-start.5 = (bf16[3,3,256,512]{3,2,1,0:T(8,128)(2,1)S(1)}, bf16[3,3,256,512]{3,2,1,0:T(8,128)(2,1)}, u32[]{:S(2)}) copy-start(bf16[3,3,256,512]{3,2,1,0:T(8,128)(2,1)} %param.7) | copy-start | bytes 7077892
  59.4 13.9 %collective-permute-start = (bf16[1,32,256]{2,1,0:T(8,128)(2,1)S(1)}, bf16[1,32,256]{2,1,0:T(8,128)(2,1)S(1)}, u32[]{:S(2)}, u32[]{:S(2)}) collective-permute-start(bf16[1,32,256]{2,1,0:T(8,128)(2,1)S(1)} %get-tuple-element.54), channel_id=1, source_target_pairs={{0,2},{2,4},{4,6},{6,8},{8,10},{10,12},{12,14},{14,16},{16,18},{18... | collective-permute-start | bytes 49160 | tf_op jit(solution)/shard_map/ppermute | solution.py:12
  61.3 12.0 %collective-permute-start.1 = (bf16[1,32,256]{2,1,0:T(8,128)(2,1)S(1)}, bf16[1,32,256]{2,1,0:T(8,128)(2,1)S(1)}, u32[]{:S(2)}, u32[]{:S(2)}) collective-permute-start(bf16[1,32,256]{2,1,0:T(8,128)(2,1)S(1)} %get-tuple-element.55), channel_id=1, source_target_pairs={{2,0},{4,2},{6,4},{8,6},{10,8},{12,10},{14,12},{16,14},{18,16},{20... | collective-permute-start | bytes 49160 | tf_op jit(solution)/shard_map/ppermute | solution.py:15
  66.5 11.5 %collective-permute-start.4 = (bf16[1,32,512]{2,1,0:T(8,128)(2,1)S(1)}, bf16[1,32,512]{2,1,0:T(8,128)(2,1)S(1)}, u32[]{:S(2)}, u32[]{:S(2)}) collective-permute-start(bf16[1,32,512]{2,1,0:T(8,128)(2,1)S(1)} %get-tuple-element.40), channel_id=1, source_target_pairs={{0,2},{2,4},{4,6},{6,8},{8,10},{10,12},{12,14},{14,16},{16,18},{18... | collective-permute-start | bytes 98312 | tf_op jit(solution)/shard_map/ppermute | solution.py:12
  68.5 9.6 %collective-permute-start.5 = (bf16[1,32,512]{2,1,0:T(8,128)(2,1)S(1)}, bf16[1,32,512]{2,1,0:T(8,128)(2,1)S(1)}, u32[]{:S(2)}, u32[]{:S(2)}) collective-permute-start(bf16[1,32,512]{2,1,0:T(8,128)(2,1)S(1)} %get-tuple-element.41), channel_id=1, source_target_pairs={{2,0},{4,2},{6,4},{8,6},{10,8},{12,10},{14,12},{16,14},{18,16},{20... | collective-permute-start | bytes 98312 | tf_op jit(solution)/shard_map/ppermute | solution.py:15
  76.5 7.6 %copy-start.19 = (f32[512,512]{1,0:T(8,128)}, f32[512,512]{1,0:T(8,128)S(1)}, u32[]{:S(2)}) copy-start(f32[512,512]{1,0:T(8,128)S(1)} %fusion.6) | copy-start | bytes 3145732
  76.5 2.9 slice-start
  78.0 1.7 slice-start.1
  84.6 3.0 copy-start.6
  84.6 17.8 %copy-start.8 = (bf16[16,32,512]{2,1,0:T(8,128)(2,1)}, bf16[16,32,512]{2,1,0:T(8,128)(2,1)S(1)}, u32[]{:S(2)}) copy-start(bf16[16,32,512]{2,1,0:T(8,128)(2,1)S(1)} %get-tuple-element.14) | copy-start | bytes 1572868
  88.3 24.8 %collective-permute-start.2 = (bf16[1,32,512]{2,1,0:T(8,128)(2,1)}, bf16[1,32,512]{2,1,0:T(8,128)(2,1)S(1)}, u32[]{:S(2)}, u32[]{:S(2)}) collective-permute-start(bf16[1,32,512]{2,1,0:T(8,128)(2,1)} %get-tuple-element.44), channel_id=1, source_target_pairs={{0,2},{2,4},{4,6},{6,8},{8,10},{10,12},{12,14},{14,16},{16,18},{18... | collective-permute-start | bytes 98312 | tf_op jit(solution)/shard_map/ppermute | solution.py:12
  90.2 22.9 %collective-permute-start.3 = (bf16[1,32,512]{2,1,0:T(8,128)(2,1)}, bf16[1,32,512]{2,1,0:T(8,128)(2,1)S(1)}, u32[]{:S(2)}, u32[]{:S(2)}) collective-permute-start(bf16[1,32,512]{2,1,0:T(8,128)(2,1)} %get-tuple-element.45), channel_id=1, source_target_pairs={{2,0},{4,2},{6,4},{8,6},{10,8},{12,10},{14,12},{16,14},{18,16},{20... | collective-permute-start | bytes 98312 | tf_op jit(solution)/shard_map/ppermute | solution.py:15
  95.0 20.3 %collective-permute-start.6 = (bf16[1,32,512]{2,1,0:T(8,128)(2,1)}, bf16[1,32,512]{2,1,0:T(8,128)(2,1)S(1)}, u32[]{:S(2)}, u32[]{:S(2)}) collective-permute-start(bf16[1,32,512]{2,1,0:T(8,128)(2,1)} %get-tuple-element.36), channel_id=1, source_target_pairs={{0,2},{2,4},{4,6},{6,8},{8,10},{10,12},{12,14},{14,16},{16,18},{18... | collective-permute-start | bytes 98312 | tf_op jit(solution)/shard_map/ppermute | solution.py:12
  97.0 18.4 %collective-permute-start.7 = (bf16[1,32,512]{2,1,0:T(8,128)(2,1)}, bf16[1,32,512]{2,1,0:T(8,128)(2,1)S(1)}, u32[]{:S(2)}, u32[]{:S(2)}) collective-permute-start(bf16[1,32,512]{2,1,0:T(8,128)(2,1)} %get-tuple-element.37), channel_id=1, source_target_pairs={{2,0},{4,2},{6,4},{8,6},{10,8},{12,10},{14,12},{16,14},{18,16},{20... | collective-permute-start | bytes 98312 | tf_op jit(solution)/shard_map/ppermute | solution.py:15
  105.8 7.3 %copy-start.7 = (bf16[16,32,512]{2,1,0:T(8,128)(2,1)S(1)}, bf16[16,32,512]{2,1,0:T(8,128)(2,1)}, u32[]{:S(2)}) copy-start(bf16[16,32,512]{2,1,0:T(8,128)(2,1)} %copy-done.6) | copy-start | bytes 1572868
  113.4 2.0 copy-start.9
  120.8 152.5 %all-reduce.11.cloned.1.call-start = ((), (), s32[]{:S(2)}) async-start(), calls=%async_computation.1 | async-start | bytes 2097152 | tf_op jit(solution)/shard_map/psum | solution.py:104
  120.9 2.4 copy-start.17
  120.9 1.9 copy-start.11
  121.4 1.9 copy-start.10
  122.9 1.9 copy-start.12
  123.3 1.9 copy-start.13
  125.7 2.0 copy-start.24
  165.8 333.9 %all-reduce.13.cloned.1.call-start = ((), (), s32[]{:S(2)}) async-start(), calls=%async_computation.2 | async-start | bytes 37748736
  166.1 2.8 copy-start.3
  166.1 3.8 copy-start.4
  188.5 1.7 copy-start.15
  188.5 3.2 copy-start.18
  194.7 1.6 copy-start.21
  200.8 302.0 %copy-start.1 = (bf16[2048,256]{1,0:T(8,128)(2,1)S(1)}, bf16[2048,256]{1,0:T(8,128)(2,1)}, u32[]{:S(2)}) copy-start(bf16[2048,256]{1,0:T(8,128)(2,1)} %param.6) | copy-start | bytes 3145732
  (6 other events, 7.7 us)
Sparse Core Ops, SparseCore 0:
  120.9 37.8 all-gather.1
  166.0 107.2 all-reduce.10
  278.8 220.8 all-reduce.12
where the time goes:
time: 511 us; the launch traced here: 509 us
  waiting for transfers between devices  322 us (63%)
  matrix products  49.1 us (10%)
  blocking collectives  44.1 us (9%)
  local copies, waits for them, and re-layouts  36.6 us (7%)
  starting transfers between devices  27.9 us (5%)
  other arithmetic  15.2 us (3%)
  between operations  14.6 us (3%)
    unnamed x4, waiting for transfers between devices  224 us
    psum x1, waiting for transfers between devices, on_device(): lax.psum(code_terms.astype(jnp.bfloat16), ('space', 'clip'))  70.1 us
    psum x1, blocking collectives, on_device(): summed = lax.psum(partial_value, 'code')  44.1 us
    all_gather x1, waiting for transfers between devices, on_device(): piece = lax.all_gather(grad_embedded, 'code', axis=0, tiled=True)  27.6 us
    another operation x2, local copies, waits for them, and re-layouts, kernel_grad(): return jnp.stack(result)  21.1 us
    ppermute x4, starting transfers between devices, with_halo(): lax.ppermute(lax.slice_in_dim(block, 0, width, axis=dim), axis, backward)  19.9 us
    dot_general x18, matrix products, taps_forward(): jnp.dot(window, kernel[first, second], preferred_element_type=jnp.float32)  17.2 us
    another operation x6, other arithmetic, kernel_grad(): return jnp.stack(result)  13.6 us
  transfers between devices with their start and end apart: 11, of which 3 were waited for; matrix products, arithmetic and copies ran while one was open for 13% of the time, Pallas kernels for 0%

commit v1 on v0

--- a/solution.py
+++ b/solution.py
@@ -2,6 +2,7 @@
 import jax.numpy as jnp
 from jax import lax
 from jax.sharding import PartitionSpec as P
+from jax.lax import axis_size, ppermute
 
 
 def with_halo(block, sides, width):
@@ -82,7 +83,15 @@
         weights.reshape(-1, code_slice), codebook, preferred_element_type=jnp.float32
     )
     partial_value = partial_value.reshape(weights.shape[0], breadth, -1)
-    summed = lax.psum(partial_value, "code")
+    fan = axis_size("code")
+    summed, current_block = (partial_value, 0)
+    while 1 << current_block < fan:
+        buffer = []
+        for tick in tuple(range(fan)):
+            buffer.append((tick, tick ^ 1 << current_block))
+        outer = ppermute(summed, axis_name="code", perm=buffer)
+        summed = summed + outer
+        current_block = current_block + 1
     owned = lax.dynamic_slice_in_dim(summed, lax.axis_index("code") * own_rows, own_rows, 0)
     embedded = owned.astype(jnp.bfloat16)
     embed_pad = extend(embedded)

time: 511 us -> 553 us (1.082)
  waiting for transfers between devices: 322 us -> 396 us
  blocking collectives: 44.1 us -> 0 us
  starting transfers between devices: 27.9 us -> 35.5 us
    psum x1 -> x0, blocking collectives: 44.1 us -> none  [on_device(): summed = lax.psum(partial_value, 'code')]
    ppermute x0 -> x2, waiting for transfers between devices: none -> 41.2 us  [on_device(): outer = ppermute(summed, axis_name='code', perm=buffer)]
    ppermute x4, waiting for transfers between devices: 0.01 us -> 38.3 us  [with_halo(): lax.ppermute(lax.slice_in_dim(block, block.shape[dim] - width, None, axis...]
    all_gather x1, waiting for transfers between devices: 27.6 us -> 21 us  [on_device(): piece = lax.all_gather(grad_embedded, 'code', axis=0, tiled=True)]
    ppermute x0 -> x2, starting transfers between devices: none -> 5.67 us  [on_device(): outer = ppermute(summed, axis_name='code', perm=buffer)]
    unnamed x59 -> x49, local copies, waits for them, and re-layouts: 9.85 us -> 13.5 us
  transfers between devices with their start and end apart: 11 -> 13, of which waited for: 3 -> 7; matrix products, arithmetic and copies ran while one was open for 13% -> 12% of each run, Pallas kernels for 0% -> 0%
where the time goes in v1:
time: 553 us; the launch traced here: 552 us
  waiting for transfers between devices  396 us (72%)
  matrix products  50.5 us (9%)
  local copies, waits for them, and re-layouts  37.5 us (7%)
  starting transfers between devices  35.5 us (6%)
  other arithmetic  17.9 us (3%)
  between operations  14.5 us (3%)
    unnamed x4, waiting for transfers between devices  224 us
    psum x1, waiting for transfers between devices, on_device(): lax.psum(code_terms.astype(jnp.bfloat16), ('space', 'clip'))  70.1 us
    ppermute x2, waiting for transfers between devices, on_device(): outer = ppermute(summed, axis_name='code', perm=buffer)  41.2 us
    ppermute x4, waiting for transfers between devices, with_halo(): lax.ppermute(lax.slice_in_dim(block, block.shape[dim] - width, None, axis...  38.3 us
    another operation x2, local copies, waits for them, and re-layouts, kernel_grad(): return jnp.stack(result)  21.1 us
    ppermute x4, starting transfers between devices, with_halo(): lax.ppermute(lax.slice_in_dim(block, 0, width, axis=dim), axis, backward)  21.1 us
    all_gather x1, waiting for transfers between devices, on_device(): piece = lax.all_gather(grad_embedded, 'code', axis=0, tiled=True)  21 us
    dot_general x18, matrix products, taps_forward(): jnp.dot(window, kernel[first, second], preferred_element_type=jnp.float32)  17.2 us
  transfers between devices with their start and end apart: 13, of which 7 were waited for; matrix products, arithmetic and copies ran while one was open for 12% of the time, Pallas kernels for 0%

profile of v1, /device:TPU:1, one launch (start us, length us, event | category | flops | bytes accessed | tf_op | source)
XLA Modules:
  0.0 551.9 jit_solution(4143290019337486907)
XLA Ops:
  8.4 7.1 %fusion = f32[64,32,256]{2,1,0:T(8,128)} fusion(bf16[1,64,32,2048]{3,2,1,0:T(8,128)(2,1)} %param.5, bf16[2048,256]{1,0:T(8,128)(2,1)S(1)} %copy-done), kind=kOutput, calls=%fused_computation.1 | convolution fusion | flops 2147483648 | bytes 11534336 | tf_op jit(solution)/shard_map/dot_general | solution.py:82
  15.5 2.5 collective-permute-start
  17.9 1.9 collective-permute-start.6
  19.8 5.0 collective-permute-start.7
  24.9 38.3 %collective-permute-done.6 = bf16[1,32,512]{2,1,0:T(8,128)(2,1)S(1)} collective-permute-done((bf16[1,32,512]{2,1,0:T(8,128)(2,1)S(1)}, bf16[1,32,512]{2,1,0:T(8,128)(2,1)S(1)}, u32[]{:S(2)}, u32[]{:S(2)}) %collective-permute-start.6) | collective-permute-done | bytes 32800 | tf_op jit(solution)/shard_map/ppermute | solution.py:13
  65.1 1.8 copy-done.3
  67.4 2.6 add.134
  70.0 3.2 collective-permute-start.1
  76.6 41.2 %collective-permute-done.1 = f32[64,32,256]{2,1,0:T(8,128)S(1)} collective-permute-done((f32[64,32,256]{2,1,0:T(8,128)S(1)}, f32[64,32,256]{2,1,0:T(8,128)S(1)}, u32[]{:S(2)}, u32[]{:S(2)}) %collective-permute-start.1) | collective-permute-done | bytes 2097184 | tf_op jit(solution)/shard_map/ppermute | solution.py:92
  117.9 2.6 collective-permute-start.2
  120.6 6.2 %collective-permute-start.3 = (bf16[1,32,256]{2,1,0:T(8,128)(2,1)S(1)}, bf16[1,32,256]{2,1,0:T(8,128)(2,1)S(1)}, u32[]{:S(2)}, u32[]{:S(2)}) collective-permute-start(bf16[1,32,256]{2,1,0:T(8,128)(2,1)S(1)} %get-tuple-element.55), channel_id=1, source_target_pairs={{2,0},{4,2},{6,4},{8,6},{10,8},{12,10},{14,12},{16,14},{18,16},{20... | collective-permute-start | bytes 49160 | tf_op jit(solution)/shard_map/ppermute | solution.py:16
  132.1 1.5 convolution_bitcast_fusion.4
  136.5 1.9 collective-permute-start.4
  138.4 4.9 collective-permute-start.5
  143.3 1.9 collective-permute-start.8
  145.2 5.0 collective-permute-start.9
  151.3 2.7 pad_maximum_fusion.1
  154.0 7.3 %copy.12 = f32[3,3,256,512]{2,1,0,3:T(4,128)} copy(f32[3,3,256,512]{3,2,1,0:T(8,128)} %pad_maximum_fusion.1) | data formatting | bytes 9437184 | tf_op jit(solution)/shard_map/stack | solution.py:73
  161.5 1.6 fusion.115
  177.0 3.4 maximum_bitcast_fusion
  180.4 21.0 %all-gather.2.cloned.1.call-done = bf16[64,32,256]{2,1,0:T(8,128)(2,1)} async-done(((bf16[16,32,256]{2,1,0:T(8,128)(2,1)}), bf16[64,32,256]{2,1,0:T(8,128)(2,1)}) %all-gather.2.cloned.1.call-update) | async-done | bytes 1048592 | tf_op jit(solution)/shard_map/all_gather | solution.py:106
  201.4 7.1 %fusion.2 = bf16[2048,256]{0,1:T(8,128)(2,1)} fusion(bf16[2048,256]{1,0:T(8,128)(2,1)} %bitcast.295, bf16[2048,2048]{1,0:T(8,128)(2,1)} %bitcast.275), kind=kOutput, calls=%fused_computation.8 | convolution fusion | flops 2148007936 | bytes 10485760 | tf_op jit(solution)/shard_map/dot_general | solution.py:107
  208.7 2.3 maximum_bitcast_fusion.2
  212.5 4.7 pad_maximum_fusion
  217.2 13.8 %copy.13 = f32[3,3,512,512]{2,1,0,3:T(4,128)} copy(f32[3,3,512,512]{3,2,1,0:T(8,128)} %pad_maximum_fusion) | data formatting | bytes 18874368 | tf_op jit(solution)/shard_map/stack | solution.py:73
  231.1 1.7 fusion.33
  237.3 1.6 convolution_add_fusion.11
  238.9 1.5 convolution_add_fusion.10
  243.4 2.4 fusion.7
  245.8 70.1 %all-reduce.10.cloned.1.call-done = bf16[2048,256]{0,1:T(8,128)(2,1)} async-done(((bf16[2048,256]{0,1:T(8,128)(2,1)}), bf16[2048,256]{0,1:T(8,128)(2,1)}) %all-reduce.10.cloned.1.call-update) | async-done | bytes 1048592 | tf_op jit(solution)/shard_map/psum | solution.py:113
  315.9 2.6 copy.16
  318.5 223.9 %all-reduce.12.cloned.1.call-done = (f32[3,3,256,512]{2,1,0,3:T(4,128)}, f32[3,3,512,512]{2,1,0,3:T(4,128)}) async-done(((f32[3,3,256,512]{2,1,0,3:T(4,128)}, f32[3,3,512,512]{2,1,0,3:T(4,128)}), (f32[3,3,256,512]{2,1,0,3:T(4,128)}, f32[3,3,512,512]{2,1,0,3:T(4,128)})) %all-reduce.12.cloned.1.call-update) | async-done | bytes 14155792
  (129 shorter events, 42.1 us)
Async XLA Ops:
  7.2 1.2 copy-start
  7.2 10.7 %copy-start.2 = (bf16[1,16,32,512]{3,2,1,0:T(8,128)(2,1)S(1)}, bf16[1,16,32,512]{3,2,1,0:T(8,128)(2,1)}, u32[]{:S(2)}) copy-start(bf16[1,16,32,512]{3,2,1,0:T(8,128)(2,1)} %param.9) | copy-start | bytes 1572868
  7.2 194.2 %all-gather.2.cloned.1.call-start = ((), (), s32[]{:S(2)}) async-start(), calls=%async_computation | async-start | bytes 1310720 | tf_op jit(solution)/shard_map/all_gather | solution.py:106
  15.5 52.0 %collective-permute-start = (f32[64,32,256]{2,1,0:T(8,128)}, f32[64,32,256]{2,1,0:T(8,128)}, u32[]{:S(2)}, u32[]{:S(2)}) collective-permute-start(f32[64,32,256]{2,1,0:T(8,128)} %fusion), channel_id=1, source_target_pairs={{0,2},{2,0},{4,6},{6,4},{1,3},{3,1},{5,7},{7,5},{8,10},{10,8},{12,... | collective-permute-start | bytes 6291464 | tf_op jit(solution)/shard_map/ppermute | solution.py:92
  17.9 45.2 %collective-permute-start.6 = (bf16[1,32,512]{2,1,0:T(8,128)(2,1)S(1)}, bf16[1,32,512]{2,1,0:T(8,128)(2,1)S(1)}, u32[]{:S(2)}, u32[]{:S(2)}) collective-permute-start(bf16[1,32,512]{2,1,0:T(8,128)(2,1)S(1)} %get-tuple-element.40), channel_id=1, source_target_pairs={{0,2},{2,4},{4,6},{6,8},{8,10},{10,12},{12,14},{14,16},{16,18},{18... | collective-permute-start | bytes 98312 | tf_op jit(solution)/shard_map/ppermute | solution.py:13
  19.8 44.4 %collective-permute-start.7 = (bf16[1,32,512]{2,1,0:T(8,128)(2,1)S(1)}, bf16[1,32,512]{2,1,0:T(8,128)(2,1)S(1)}, u32[]{:S(2)}, u32[]{:S(2)}) collective-permute-start(bf16[1,32,512]{2,1,0:T(8,128)(2,1)S(1)} %get-tuple-element.41), channel_id=1, source_target_pairs={{2,0},{4,2},{6,4},{8,6},{10,8},{12,10},{14,12},{16,14},{18,16},{20... | collective-permute-start | bytes 98312 | tf_op jit(solution)/shard_map/ppermute | solution.py:16
  64.6 2.3 copy-start.3
  70.0 47.8 %collective-permute-start.1 = (f32[64,32,256]{2,1,0:T(8,128)S(1)}, f32[64,32,256]{2,1,0:T(8,128)S(1)}, u32[]{:S(2)}, u32[]{:S(2)}) collective-permute-start(f32[64,32,256]{2,1,0:T(8,128)S(1)} %add.134), channel_id=1, source_target_pairs={{0,4},{2,6},{4,0},{6,2},{1,5},{3,7},{5,1},{7,3},{8,12},{10,14},{12... | collective-permute-start | bytes 6291464 | tf_op jit(solution)/shard_map/ppermute | solution.py:92
  117.9 9.4 %collective-permute-start.2 = (bf16[1,32,256]{2,1,0:T(8,128)(2,1)S(1)}, bf16[1,32,256]{2,1,0:T(8,128)(2,1)S(1)}, u32[]{:S(2)}, u32[]{:S(2)}) collective-permute-start(bf16[1,32,256]{2,1,0:T(8,128)(2,1)S(1)} %get-tuple-element.54), channel_id=1, source_target_pairs={{0,2},{2,4},{4,6},{6,8},{8,10},{10,12},{12,14},{14,16},{16,18},{18... | collective-permute-start | bytes 49160 | tf_op jit(solution)/shard_map/ppermute | solution.py:13
  120.6 7.0 %collective-permute-start.3 = (bf16[1,32,256]{2,1,0:T(8,128)(2,1)S(1)}, bf16[1,32,256]{2,1,0:T(8,128)(2,1)S(1)}, u32[]{:S(2)}, u32[]{:S(2)}) collective-permute-start(bf16[1,32,256]{2,1,0:T(8,128)(2,1)S(1)} %get-tuple-element.55), channel_id=1, source_target_pairs={{2,0},{4,2},{6,4},{8,6},{10,8},{12,10},{14,12},{16,14},{18,16},{20... | collective-permute-start | bytes 49160 | tf_op jit(solution)/shard_map/ppermute | solution.py:16
  127.3 6.3 %copy-start.19 = (f32[512,512]{1,0:T(8,128)}, f32[512,512]{1,0:T(8,128)S(1)}, u32[]{:S(2)}) copy-start(f32[512,512]{1,0:T(8,128)S(1)} %fusion.4) | copy-start | bytes 3145732
  127.3 2.0 copy-start.6
  132.1 1.5 copy-start.16
  136.5 24.8 %collective-permute-start.4 = (bf16[1,32,512]{2,1,0:T(8,128)(2,1)S(1)}, bf16[1,32,512]{2,1,0:T(8,128)(2,1)S(1)}, u32[]{:S(2)}, u32[]{:S(2)}) collective-permute-start(bf16[1,32,512]{2,1,0:T(8,128)(2,1)S(1)} %get-tuple-element.44), channel_id=1, source_target_pairs={{0,2},{2,4},{4,6},{6,8},{8,10},{10,12},{12,14},{14,16},{16,18},{18... | collective-permute-start | bytes 98312 | tf_op jit(solution)/shard_map/ppermute | solution.py:13
  138.4 22.9 %collective-permute-start.5 = (bf16[1,32,512]{2,1,0:T(8,128)(2,1)S(1)}, bf16[1,32,512]{2,1,0:T(8,128)(2,1)S(1)}, u32[]{:S(2)}, u32[]{:S(2)}) collective-permute-start(bf16[1,32,512]{2,1,0:T(8,128)(2,1)S(1)} %get-tuple-element.45), channel_id=1, source_target_pairs={{2,0},{4,2},{6,4},{8,6},{10,8},{12,10},{14,12},{16,14},{18,16},{20... | collective-permute-start | bytes 98312 | tf_op jit(solution)/shard_map/ppermute | solution.py:16
  143.3 19.9 %collective-permute-start.8 = (bf16[1,32,512]{2,1,0:T(8,128)(2,1)S(1)}, bf16[1,32,512]{2,1,0:T(8,128)(2,1)S(1)}, u32[]{:S(2)}, u32[]{:S(2)}) collective-permute-start(bf16[1,32,512]{2,1,0:T(8,128)(2,1)S(1)} %get-tuple-element.36), channel_id=1, source_target_pairs={{0,2},{2,4},{4,6},{6,8},{8,10},{10,12},{12,14},{14,16},{16,18},{18... | collective-permute-start | bytes 98312 | tf_op jit(solution)/shard_map/ppermute | solution.py:13
  145.2 18.0 %collective-permute-start.9 = (bf16[1,32,512]{2,1,0:T(8,128)(2,1)S(1)}, bf16[1,32,512]{2,1,0:T(8,128)(2,1)S(1)}, u32[]{:S(2)}, u32[]{:S(2)}) collective-permute-start(bf16[1,32,512]{2,1,0:T(8,128)(2,1)S(1)} %get-tuple-element.37), channel_id=1, source_target_pairs={{2,0},{4,2},{6,4},{8,6},{10,8},{12,10},{14,12},{16,14},{18,16},{20... | collective-permute-start | bytes 98312 | tf_op jit(solution)/shard_map/ppermute | solution.py:16
  163.4 1.7 copy-start.7
  165.5 1.2 copy-start.17
  165.5 1.5 copy-start.20
  169.7 146.2 %all-reduce.10.cloned.1.call-start = ((), (), s32[]{:S(2)}) async-start(), calls=%async_computation.1 | async-start | bytes 2097152 | tf_op jit(solution)/shard_map/psum | solution.py:113
  169.9 2.3 copy-start.8
  172.1 1.9 copy-start.9
  172.6 1.9 copy-start.10
  175.0 2.0 copy-start.21
  208.5 333.9 %all-reduce.12.cloned.1.call-start = ((), (), s32[]{:S(2)}) async-start(), calls=%async_computation.2 | async-start | bytes 37748736
  208.7 2.8 copy-start.4
  208.7 3.8 copy-start.5
  231.1 1.7 copy-start.12
  231.1 3.2 copy-start.15
  237.3 1.6 copy-start.18
  243.4 302.0 %copy-start.1 = (bf16[2048,256]{1,0:T(8,128)(2,1)S(1)}, bf16[2048,256]{1,0:T(8,128)(2,1)}, u32[]{:S(2)}) copy-start(bf16[2048,256]{1,0:T(8,128)(2,1)} %param.6) | copy-start | bytes 3145732
  (3 other events, 2.9 us)
Sparse Core Ops, SparseCore 0:
  169.8 31.4 all-gather.1
  208.6 107.2 all-reduce.9
  321.5 220.8 all-reduce.11
